TPU v7x, 512 devices: a whole 4x8x8 slice. The times are simulated.
512 devices in a mesh: panel: 2 (over y_lo), lon: 16 (over z, core), lat: 16 (over y_hi, x).
Axes of the slice: x: 4, y: 8 (y_hi: 4, y_lo: 2; y = y_hi * 2 + y_lo), z: 8, core: 2. Of those that a mesh axis runs over, the one named last changes fastest.
Arguments:
- pressure: float32 [2, 256, 512, 128], P('panel', 'lat', 'lon'), may hold values from -6 to 6
- porosity: float32 [2, 256, 512, 128], P('panel', 'lat', 'lon'), may hold values from 0.5 to 2
- source: float32 [2, 256, 512, 128], P('panel', 'lat', 'lon'), may hold values from -6 to 6
- bulk: float32 [2, 256, 512, 128], P('panel', 'lat', 'lon'), may hold values from 0.5 to 2
- lat_codes: int32 [2, 2, 2, 512], P('panel', None, None, 'lon'), may hold values from 0 to 8158, as said below
- lat_weights: float32 [2, 4, 2, 2, 512], P('panel', None, None, None, 'lon'), may hold values from 0 to 1, as said below
- lon_codes: int32 [2, 2, 2, 256], P('panel', None, None, 'lat'), may hold values from 0 to 8174, as said below
- lon_weights: float32 [2, 4, 2, 2, 256], P('panel', None, None, None, 'lat'), may hold values from 0 to 1, as said below
Outputs:
- pressure_out: float32 [2, 256, 512, 128], P('panel', 'lat', 'lon')
- porosity_out: float32 [2, 256, 512, 128], P('panel', 'lat', 'lon')
Inputs may be any that keep to these rules, and one draw needn't show every extreme that they name: `lat_codes`: an intersection map of the shell, which may differ from draw to draw: code = a * 32 + c with a < 255 a latitude of the whole panel and c < 31 an offset inside the longitude block of the ghost cell. `lon_codes`: an intersection map of the shell, which may differ from draw to draw: code = b * 16 + r with b < 511 a longitude of the whole panel and r < 15 an offset inside the latitude block of the ghost cell. `lat_weights`: the four weights of a ghost cell are non-negative and sum to one. `lon_weights`: the four weights of a ghost cell are non-negative and sum to one.
All inputs are finite; a program needn't handle non-finite values.
Results may differ from a plain program's by a relative error of at most 0.0003.
Values sent between devices are 32-bit elements; how exact they have to be, the bound alone decides.
A program may use at most 64 MiB of HBM per device.

v0:
```python
import jax
import jax.numpy as jnp
from jax import lax
from jax.sharding import PartitionSpec as P

SWEEPS = 3
stencil_offsets = ((0, 0), (0, 1), (1, 0), (1, 1))
radial_weight = 0.25
buoyancy = 0.5
time_step = 0.04


def padded_2(cells, sides, width):
    for axis, dim in sides:
        count = lax.axis_size(axis)
        ends = count - 1
        head = lax.slice_in_dim(cells, 0, width, axis=dim)
        tail = lax.slice_in_dim(cells, cells.shape[dim] - width, cells.shape[dim], axis=dim)
        cells = jnp.concatenate(
            [
                lax.ppermute(tail, axis, [(i, (i + 1) % count) for i in range(ends)]),
                cells,
                lax.ppermute(head, axis, [((i + 1) % count, i) for i in range(ends)]),
            ],
            axis=dim,
        )
    return cells


def swapped(block, axis, distance):
    count = lax.axis_size(axis)
    route = []
    for low in range(count):
        high = low | 1 << distance
        if high != low and high < count:
            route += [(low, high), (high, low)]
    return lax.ppermute(block, axis, route)


def pad_last(values, before, after):
    widths = [(0, 0)] * (values.ndim - 1) + [(before, after)]
    return jnp.pad(values, widths)


def rim_terms(field, lat_codes, lat_weights, lon_codes, lon_weights, width):
    rows_dev, cols_dev, levels = field.shape
    first_row = lax.axis_index("lat") * rows_dev
    first_col = lax.axis_index("lon") * cols_dev
    chosen = lat_codes[:, :width]
    rows_at = chosen // cols_dev - first_row
    cols_at = chosen % cols_dev
    lat_total = jnp.zeros(chosen.shape + (levels,), jnp.float32)
    for corner, (row_step, col_step) in enumerate(stencil_offsets):
        target = rows_at + row_step
        inside = (target >= 0) & (target < rows_dev)
        picked = field[jnp.clip(target, 0, rows_dev - 1), cols_at + col_step]
        lat_total = (
            lat_total + jnp.where(inside, lat_weights[corner, :, :width], 0.0)[..., None] * picked
        )
    chosen = lon_codes[:, :width]
    cols_at = chosen // rows_dev - first_col
    rows_at = chosen % rows_dev
    lon_total = jnp.zeros(chosen.shape + (levels,), jnp.float32)
    for corner, (row_step, col_step) in enumerate(stencil_offsets):
        target = cols_at + col_step
        inside = (target >= 0) & (target < cols_dev)
        picked = field[rows_at + row_step, jnp.clip(target, 0, cols_dev - 1)]
        lon_total = (
            lon_total + jnp.where(inside, lon_weights[corner, :, :width], 0.0)[..., None] * picked
        )
    return (lat_total, lon_total)


def surround(field, width, lat_codes, lat_weights, lon_codes, lon_weights):
    rows_dev, cols_dev, levels = field.shape
    padded = padded_2(field, (("lat", 0), ("lon", 1)), width)
    lat_terms, lon_terms = rim_terms(field, lat_codes, lat_weights, lon_codes, lon_weights, width)
    lat_summed = lax.psum(lat_terms, "lat")
    lon_summed = lax.psum(lon_terms, "lon")
    arrived = swapped(jnp.concatenate([lat_summed, lon_summed], axis=2), "panel", 0)
    lat_rim = arrived[:, :, :cols_dev]
    lon_rim = arrived[:, :, cols_dev:]
    lat_index = lax.axis_index("lat")
    lon_index = lax.axis_index("lon")
    last_lat = lax.axis_size("lat") - 1
    last_lon = lax.axis_size("lon") - 1
    north = jnp.where(lat_index == 0, lat_rim[0][::-1], padded[:width, width : width + cols_dev])
    padded = padded.at[:width, width : width + cols_dev].set(north)
    south = jnp.where(
        lat_index == last_lat, lat_rim[1], padded[width + rows_dev :, width : width + cols_dev]
    )
    padded = padded.at[width + rows_dev :, width : width + cols_dev].set(south)
    west = jnp.where(
        lon_index == 0,
        jnp.moveaxis(lon_rim[0][::-1], 0, 1),
        padded[width : width + rows_dev, :width],
    )
    padded = padded.at[width : width + rows_dev, :width].set(west)
    east = jnp.where(
        lon_index == last_lon,
        jnp.moveaxis(lon_rim[1], 0, 1),
        padded[width : width + rows_dev, width + cols_dev :],
    )
    padded = padded.at[width : width + rows_dev, width + cols_dev :].set(east)
    return padded


def face_terms(mobility):
    lat_face = 0.5 * (mobility[..., :-1, 1:-1, :] + mobility[..., 1:, 1:-1, :])
    lon_face = 0.5 * (mobility[..., 1:-1, :-1, :] + mobility[..., 1:-1, 1:, :])
    inner = mobility[..., 1:-1, 1:-1, :]
    mean_rad = 0.5 * (inner[..., :-1] + inner[..., 1:])
    return (lat_face, lon_face, mean_rad)


def diagonal_sum(bulk, lat_face, lon_face, mean_rad):
    rad_face = radial_weight * mean_rad
    total = bulk + lat_face[..., :-1, :, :] + lat_face[..., 1:, :, :]
    total = total + lon_face[..., :, :-1, :] + lon_face[..., :, 1:, :]
    return total + pad_last(rad_face, 1, 0) + pad_last(rad_face, 0, 1)


def neighbour_total(padded, source, lat_face, lon_face, mean_rad):
    inner = padded[..., 1:-1, 1:-1, :]
    rad_face = radial_weight * mean_rad
    total = source + lat_face[..., :-1, :, :] * padded[..., :-2, 1:-1, :]
    total = total + lat_face[..., 1:, :, :] * padded[..., 2:, 1:-1, :]
    total = total + lon_face[..., :, :-1, :] * padded[..., 1:-1, :-2, :]
    total = total + lon_face[..., :, 1:, :] * padded[..., 1:-1, 2:, :]
    total = (
        total
        + pad_last(rad_face * inner[..., :-1], 1, 0)
        + pad_last(rad_face * inner[..., 1:], 0, 1)
    )
    return total


def advect(pressure_pad, porosity_pad, lat_face, lon_face, mean_rad, bulk):
    pressure_in = pressure_pad[..., 1:-1, 1:-1, :]
    porosity_in = porosity_pad[..., 2:-2, 2:-2, :]
    lat_speed = -lat_face * (pressure_pad[..., 1:, 1:-1, :] - pressure_pad[..., :-1, 1:-1, :])
    lat_left = 1.5 * porosity_pad[..., 1:-2, 2:-2, :] - 0.5 * porosity_pad[..., :-3, 2:-2, :]
    lat_right = 1.5 * porosity_pad[..., 2:-1, 2:-2, :] - 0.5 * porosity_pad[..., 3:, 2:-2, :]
    lat_flux = lat_speed * jnp.where(lat_speed > 0, lat_left, lat_right)
    lon_speed = -lon_face * (pressure_pad[..., 1:-1, 1:, :] - pressure_pad[..., 1:-1, :-1, :])
    lon_left = 1.5 * porosity_pad[..., 2:-2, 1:-2, :] - 0.5 * porosity_pad[..., 2:-2, :-3, :]
    lon_right = 1.5 * porosity_pad[..., 2:-2, 2:-1, :] - 0.5 * porosity_pad[..., 2:-2, 3:, :]
    lon_flux = lon_speed * jnp.where(lon_speed > 0, lon_left, lon_right)
    rad_speed = (
        -radial_weight * mean_rad * (pressure_in[..., 1:] - pressure_in[..., :-1])
        + buoyancy * mean_rad
    )
    rad_flux = rad_speed * jnp.where(rad_speed > 0, porosity_in[..., :-1], porosity_in[..., 1:])
    divergence = lat_flux[..., 1:, :, :] - lat_flux[..., :-1, :, :]
    divergence = divergence + lon_flux[..., :, 1:, :] - lon_flux[..., :, :-1, :]
    divergence = divergence + pad_last(rad_flux, 0, 1) - pad_last(rad_flux, 1, 0)
    return porosity_in - time_step * (divergence + bulk * pressure_in)


def body(pressure, porosity, source, bulk, lat_codes, lat_weights, lon_codes, lon_weights):
    current = pressure[0]
    porosity_now = porosity[0]
    source_now = source[0]
    bulk_now = bulk[0]
    lat_code_now = lat_codes[0]
    lat_weight_now = lat_weights[0]
    lon_code_now = lon_codes[0]
    lon_weight_now = lon_weights[0]
    levels = porosity_now.shape[-1]
    both_pad = surround(
        jnp.concatenate([porosity_now, current], axis=-1),
        2,
        lat_code_now,
        lat_weight_now,
        lon_code_now,
        lon_weight_now,
    )
    porosity_pad = both_pad[..., :levels]
    first_pad = both_pad[1:-1, 1:-1, levels:]
    near = porosity_pad[1:-1, 1:-1, :]
    mobility = near * near * near
    lat_face, lon_face, mean_rad = face_terms(mobility)
    denominator = diagonal_sum(bulk_now, lat_face, lon_face, mean_rad)
    for sweep_index in range(SWEEPS):
        if sweep_index == 0:
            padded = first_pad
        else:
            padded = surround(
                current, 1, lat_code_now, lat_weight_now, lon_code_now, lon_weight_now
            )
        current = neighbour_total(padded, source_now, lat_face, lon_face, mean_rad) / denominator
    pressure_pad = surround(current, 1, lat_code_now, lat_weight_now, lon_code_now, lon_weight_now)
    porosity_new = advect(pressure_pad, porosity_pad, lat_face, lon_face, mean_rad, bulk_now)
    return (current[None], porosity_new[None])


def solution(mesh):
    placed = (
        P("panel", "lat", "lon", None),
        P("panel", "lat", "lon", None),
        P("panel", "lat", "lon", None),
        P("panel", "lat", "lon", None),
        P("panel", None, None, "lon"),
        P("panel", None, None, None, "lon"),
        P("panel", None, None, "lat"),
        P("panel", None, None, None, "lat"),
    )
    return jax.shard_map(
        body,
        mesh=mesh,
        in_specs=placed,
        out_specs=(P("panel", "lat", "lon", None), P("panel", "lat", "lon", None)),
        check_vma=False,
    )
```

profile of v0, /device:TPU:296, one launch (start us, length us, event | category | flops | bytes accessed | tf_op | source)
XLA Modules:
  0.0 794.1 jit_solution(9546006194397543275)
XLA Ops:
  8.6 3.4 collective-permute-start
  12.0 6.7 collective-permute-start.1
  33.9 1.9 collective-permute-start.2
  35.9 4.9 collective-permute-start.3
  40.7 85.8 %all-reduce.15.cloned.1.call-done = f32[2,2,16,256]{3,2,1,0:T(8,128)} async-done(((f32[2,2,16,256]{3,2,1,0:T(8,128)}), f32[2,2,16,256]{3,2,1,0:T(8,128)}) %all-reduce.15.cloned.1.call-update) | async-done | bytes 65552 | tf_op jit(solution)/shard_map/psum | solution.py:79
  126.6 174.8 %all-reduce.13.cloned.1.call-done = f32[2,2,32,256]{3,2,1,0:T(8,128)} async-done(((f32[2,2,32,256]{3,2,1,0:T(8,128)}), f32[2,2,32,256]{3,2,1,0:T(8,128)}) %all-reduce.13.cloned.1.call-update) | async-done | bytes 131088 | tf_op jit(solution)/shard_map/psum | solution.py:78
  302.3 3.4 collective-permute-start.4
  307.0 2.8 collective-permute-done.4
  310.2 1.9 dynamic-slice_select_fusion
  316.4 6.1 collective-permute-start.6
  325.3 1.9 collective-permute-start.5
  330.9 82.9 %psum.58 = f32[2,1,32,128]{3,2,1,0:T(8,128)S(1)} all-reduce(f32[2,1,32,128]{3,2,1,0:T(8,128)S(1)} %multiply_add_fusion.4), channel_id=1, replica_groups=mesh['panel'=2,'lon'=16,'lat'=16] {'lat'}, use_global_device_ids=true, to_apply=%region_3.4 | all-reduce | flops 8192 | bytes 65536 | tf_op jit(solution)/shard_map/psum | solution.py:78
  413.9 45.7 %psum.59 = f32[2,1,16,128]{3,2,1,0:T(8,128)S(1)} all-reduce(f32[2,1,16,128]{3,2,1,0:T(8,128)S(1)} %multiply_add_fusion.7), channel_id=1, replica_groups=mesh['panel'=2,'lon'=16,'lat'=16] {'lon'}, use_global_device_ids=true, to_apply=%region_4.5 | all-reduce | flops 4096 | bytes 32768 | tf_op jit(solution)/shard_map/psum | solution.py:79
  459.6 2.1 collective-permute-start.7
  461.8 4.9 collective-permute-start.8
  466.6 2.4 collective-permute-start.9
  469.2 3.5 collective-permute-done.9
  482.5 1.9 collective-permute-start.11
  484.5 3.9 collective-permute-start.10
  488.5 80.9 %psum.60 = f32[2,1,32,128]{3,2,1,0:T(8,128)S(1)} all-reduce(f32[2,1,32,128]{3,2,1,0:T(8,128)S(1)} %multiply_add_fusion.3), channel_id=1, replica_groups=mesh['panel'=2,'lon'=16,'lat'=16] {'lat'}, use_global_device_ids=true, to_apply=%region_5.6 | all-reduce | flops 8192 | bytes 65536 | tf_op jit(solution)/shard_map/psum | solution.py:78
  569.5 45.7 %psum.61 = f32[2,1,16,128]{3,2,1,0:T(8,128)S(1)} all-reduce(f32[2,1,16,128]{3,2,1,0:T(8,128)S(1)} %multiply_add_fusion.6), channel_id=1, replica_groups=mesh['panel'=2,'lon'=16,'lat'=16] {'lon'}, use_global_device_ids=true, to_apply=%region_6.7 | all-reduce | flops 4096 | bytes 32768 | tf_op jit(solution)/shard_map/psum | solution.py:79
  615.2 1.9 collective-permute-start.12
  617.2 4.9 collective-permute-start.13
  622.0 2.4 collective-permute-start.14
  624.6 3.5 collective-permute-done.14
  638.0 1.9 collective-permute-start.16
  639.9 3.9 collective-permute-start.15
  643.9 80.9 %psum.62 = f32[2,1,32,128]{3,2,1,0:T(8,128)S(1)} all-reduce(f32[2,1,32,128]{3,2,1,0:T(8,128)S(1)} %multiply_add_fusion.2), channel_id=1, replica_groups=mesh['panel'=2,'lon'=16,'lat'=16] {'lat'}, use_global_device_ids=true, to_apply=%region_7.8 | all-reduce | flops 8192 | bytes 65536 | tf_op jit(solution)/shard_map/psum | solution.py:78
  724.9 45.7 %psum.63 = f32[2,1,16,128]{3,2,1,0:T(8,128)S(1)} all-reduce(f32[2,1,16,128]{3,2,1,0:T(8,128)S(1)} %multiply_add_fusion.5), channel_id=1, replica_groups=mesh['panel'=2,'lon'=16,'lat'=16] {'lon'}, use_global_device_ids=true, to_apply=%region_8.9 | all-reduce | flops 4096 | bytes 32768 | tf_op jit(solution)/shard_map/psum | solution.py:79
  772.6 4.9 collective-permute-start.18
  777.5 2.4 collective-permute-start.19
  780.8 2.7 collective-permute-done.19
  (210 shorter events, 56.5 us)
Async XLA Ops:
  7.2 119.4 %all-reduce.15.cloned.1.call-start = ((), (), s32[]{:S(2)}) async-start(), calls=%async_computation.1 | async-start | bytes 131072 | tf_op jit(solution)/shard_map/psum | solution.py:79
  8.6 25.3 %collective-permute-start = (f32[2,32,256]{2,0,1:T(2,128)S(1)}, f32[2,32,256]{2,0,1:T(2,128)S(1)}, u32[]{:S(2)}, u32[]{:S(2)}) collective-permute-start(f32[2,32,256]{2,0,1:T(2,128)S(1)} %get-tuple-element.224), channel_id=1, source_target_pairs={{0,1},{1,2},{2,3},{3,4},{4,5},{5,6},{6,7},{7,8},{8,9},{9,10},{10,1... | collective-permute-start | bytes 196616 | tf_op jit(solution)/shard_map/ppermute | solution.py:21
  12.0 21.9 %collective-permute-start.1 = (f32[2,32,256]{2,0,1:T(2,128)S(1)}, f32[2,32,256]{2,0,1:T(2,128)S(1)}, u32[]{:S(2)}, u32[]{:S(2)}) collective-permute-start(f32[2,32,256]{2,0,1:T(2,128)S(1)} %get-tuple-element.225), channel_id=1, source_target_pairs={{1,0},{2,1},{3,2},{4,3},{5,4},{6,5},{7,6},{8,7},{9,8},{10,9},{11,1... | collective-permute-start | bytes 196616 | tf_op jit(solution)/shard_map/ppermute | solution.py:23
  18.7 0.7 copy-start.6
  18.7 0.7 copy-start.4
  24.5 0.7 copy-start.7
  24.5 0.7 copy-start.5
  24.5 276.8 %all-reduce.13.cloned.1.call-start = ((), (), s32[]{:S(2)}) async-start(), calls=%async_computation | async-start | bytes 262144 | tf_op jit(solution)/shard_map/psum | solution.py:78
  31.9 0.7 copy-start.8
  33.9 273.0 %collective-permute-start.2 = (f32[20,2,256]{2,0,1:T(8,128)S(1)}, f32[20,2,256]{2,0,1:T(8,128)S(1)}, u32[]{:S(2)}, u32[]{:S(2)}) collective-permute-start(f32[20,2,256]{2,0,1:T(8,128)S(1)} %get-tuple-element.222), channel_id=1, source_target_pairs={{0,16},{16,32},{32,48},{48,64},{64,80},{80,96},{96,112},{112,128},... | collective-permute-start | bytes 122888 | tf_op jit(solution)/shard_map/ppermute | solution.py:21
  35.9 271.0 %collective-permute-start.3 = (f32[20,2,256]{2,0,1:T(8,128)S(1)}, f32[20,2,256]{2,0,1:T(8,128)S(1)}, u32[]{:S(2)}, u32[]{:S(2)}) collective-permute-start(f32[20,2,256]{2,0,1:T(8,128)S(1)} %get-tuple-element.223), channel_id=1, source_target_pairs={{16,0},{32,16},{48,32},{64,48},{80,64},{96,80},{112,96},{128,112},... | collective-permute-start | bytes 122888 | tf_op jit(solution)/shard_map/ppermute | solution.py:23
  302.3 7.6 collective-permute-start.4
  314.7 1.0 copy-start
  314.7 1.0 copy-start.1
  316.4 143.2 %collective-permute-start.6 = (f32[1,32,128]{2,0,1:T(1,128)S(1)}, f32[1,32,128]{2,0,1:T(1,128)S(1)}, u32[]{:S(2)}, u32[]{:S(2)}) collective-permute-start(f32[1,32,128]{2,0,1:T(1,128)S(1)} %slice.1083), channel_id=1, source_target_pairs={{1,0},{2,1},{3,2},{4,3},{5,4},{6,5},{7,6},{8,7},{9,8},{10,9},{11,1... | collective-permute-start | bytes 49160 | tf_op jit(solution)/shard_map/ppermute | solution.py:23
  325.3 134.3 %collective-permute-start.5 = (f32[1,32,128]{2,1,0:T(8,128)S(1)}, f32[1,32,128]{2,1,0:T(8,128)S(1)}, u32[]{:S(2)}, u32[]{:S(2)}) collective-permute-start(f32[1,32,128]{2,1,0:T(8,128)S(1)} %slice.1082), channel_id=1, source_target_pairs={{0,1},{1,2},{2,3},{3,4},{4,5},{5,6},{6,7},{7,8},{8,9},{9,10},{10,1... | collective-permute-start | bytes 49160 | tf_op jit(solution)/shard_map/ppermute | solution.py:21
  459.6 9.4 %collective-permute-start.7 = (f32[18,1,128]{2,0,1:T(8,128)S(1)}, f32[18,1,128]{2,0,1:T(8,128)S(1)}, u32[]{:S(2)}, u32[]{:S(2)}) collective-permute-start(f32[18,1,128]{2,0,1:T(8,128)S(1)} %get-tuple-element.230), channel_id=1, source_target_pairs={{0,16},{16,32},{32,48},{48,64},{64,80},{80,96},{96,112},{112,128},... | collective-permute-start | bytes 27656 | tf_op jit(solution)/shard_map/ppermute | solution.py:21
  461.8 7.3 collective-permute-start.8
  466.6 6.0 collective-permute-start.9
  474.6 1.0 copy-start.2
  482.5 132.7 %collective-permute-start.11 = (f32[1,32,128]{2,0,1:T(1,128)S(1)}, f32[1,32,128]{2,0,1:T(1,128)S(1)}, u32[]{:S(2)}, u32[]{:S(2)}) collective-permute-start(f32[1,32,128]{2,0,1:T(1,128)S(1)} %slice.1124), channel_id=1, source_target_pairs={{1,0},{2,1},{3,2},{4,3},{5,4},{6,5},{7,6},{8,7},{9,8},{10,9},{11,1... | collective-permute-start | bytes 49160 | tf_op jit(solution)/shard_map/ppermute | solution.py:23
  484.5 130.7 %collective-permute-start.10 = (f32[1,32,128]{2,1,0:T(8,128)S(1)}, f32[1,32,128]{2,1,0:T(8,128)S(1)}, u32[]{:S(2)}, u32[]{:S(2)}) collective-permute-start(f32[1,32,128]{2,1,0:T(8,128)S(1)} %slice.1123), channel_id=1, source_target_pairs={{0,1},{1,2},{2,3},{3,4},{4,5},{5,6},{6,7},{7,8},{8,9},{9,10},{10,1... | collective-permute-start | bytes 49160 | tf_op jit(solution)/shard_map/ppermute | solution.py:21
  615.2 9.2 %collective-permute-start.12 = (f32[18,1,128]{2,0,1:T(8,128)S(1)}, f32[18,1,128]{2,0,1:T(8,128)S(1)}, u32[]{:S(2)}, u32[]{:S(2)}) collective-permute-start(f32[18,1,128]{2,0,1:T(8,128)S(1)} %get-tuple-element.228), channel_id=1, source_target_pairs={{0,16},{16,32},{32,48},{48,64},{64,80},{80,96},{96,112},{112,128},... | collective-permute-start | bytes 27656 | tf_op jit(solution)/shard_map/ppermute | solution.py:21
  617.2 7.3 collective-permute-start.13
  622.0 6.0 collective-permute-start.14
  630.0 1.0 copy-start.3
  638.0 132.7 %collective-permute-start.16 = (f32[1,32,128]{2,0,1:T(1,128)S(1)}, f32[1,32,128]{2,0,1:T(1,128)S(1)}, u32[]{:S(2)}, u32[]{:S(2)}) collective-permute-start(f32[1,32,128]{2,0,1:T(1,128)S(1)} %slice.1140), channel_id=1, source_target_pairs={{1,0},{2,1},{3,2},{4,3},{5,4},{6,5},{7,6},{8,7},{9,8},{10,9},{11,1... | collective-permute-start | bytes 49160 | tf_op jit(solution)/shard_map/ppermute | solution.py:23
  639.9 130.7 %collective-permute-start.15 = (f32[1,32,128]{2,1,0:T(8,128)S(1)}, f32[1,32,128]{2,1,0:T(8,128)S(1)}, u32[]{:S(2)}, u32[]{:S(2)}) collective-permute-start(f32[1,32,128]{2,1,0:T(8,128)S(1)} %slice.1139), channel_id=1, source_target_pairs={{0,1},{1,2},{2,3},{3,4},{4,5},{5,6},{6,7},{7,8},{8,9},{9,10},{10,1... | collective-permute-start | bytes 49160 | tf_op jit(solution)/shard_map/ppermute | solution.py:21
  770.7 10.0 %collective-permute-start.17 = (f32[18,1,128]{2,0,1:T(8,128)S(1)}, f32[18,1,128]{2,0,1:T(8,128)S(1)}, u32[]{:S(2)}, u32[]{:S(2)}) collective-permute-start(f32[18,1,128]{2,0,1:T(8,128)S(1)} %get-tuple-element.226), channel_id=1, source_target_pairs={{0,16},{16,32},{32,48},{48,64},{64,80},{80,96},{96,112},{112,128},... | collective-permute-start | bytes 27656 | tf_op jit(solution)/shard_map/ppermute | solution.py:21
  772.6 8.1 %collective-permute-start.18 = (f32[18,1,128]{2,0,1:T(8,128)S(1)}, f32[18,1,128]{2,0,1:T(8,128)S(1)}, u32[]{:S(2)}, u32[]{:S(2)}) collective-permute-start(f32[18,1,128]{2,0,1:T(8,128)S(1)} %get-tuple-element.227), channel_id=1, source_target_pairs={{16,0},{32,16},{48,32},{64,48},{80,64},{96,80},{112,96},{128,112},... | collective-permute-start | bytes 27656 | tf_op jit(solution)/shard_map/ppermute | solution.py:23
  777.5 6.0 collective-permute-start.19
Sparse Core Ops, SparseCore 0:
  24.6 101.8 all-reduce.14
  130.0 171.2 all-reduce.12
where the time goes:
time: 795 us; the launch traced here: 794 us
  blocking collectives  382 us (48%)
  waiting for transfers between devices  273 us (34%)
  starting transfers between devices  67.7 us (9%)
  local copies, waits for them, and re-layouts  46.2 us (6%)
  between operations  15.1 us (2%)
  other arithmetic  10.1 us (1%)
    psum x3, blocking collectives, surround(): lat_summed = lax.psum(lat_terms, 'lat')  245 us
    psum x1, waiting for transfers between devices, surround(): lat_summed = lax.psum(lat_terms, 'lat')  175 us
    psum x3, blocking collectives, surround(): lon_summed = lax.psum(lon_terms, 'lon')  137 us
    psum x1, waiting for transfers between devices, surround(): lon_summed = lax.psum(lon_terms, 'lon')  85.8 us
    ppermute x8, starting transfers between devices, padded_2(): lax.ppermute(head, axis, [((i + 1) % count, i) for i in range(ends)])  36 us
    ppermute x8, starting transfers between devices, padded_2(): lax.ppermute(tail, axis, [(i, (i + 1) % count) for i in range(ends)])  21 us
  transfers between devices with their start and end apart: 22, of which 6 were waited for; matrix products, arithmetic and copies ran while one was open for 3% of the time, Pallas kernels for 0%

commit v1 on v0

--- a/solution.py
+++ b/solution.py
@@ -76,7 +76,7 @@
     padded = padded_2(field, (("lat", 0), ("lon", 1)), width)
     lat_terms, lon_terms = rim_terms(field, lat_codes, lat_weights, lon_codes, lon_weights, width)
     lat_summed = lax.psum(lat_terms, "lat")
-    lon_summed = lax.psum(lon_terms, "lon")
+    lon_summed = jnp.sum(lax.all_gather(lon_terms, "lon"), axis=0)
     arrived = swapped(jnp.concatenate([lat_summed, lon_summed], axis=2), "panel", 0)
     lat_rim = arrived[:, :, :cols_dev]
     lon_rim = arrived[:, :, cols_dev:]

time: 795 us -> 606 us (0.76)
  the two profiles are of different devices: /device:TPU:296 before, /device:TPU:104 now
where the time goes in v1:
time: 606 us; the launch traced here: 605 us
  blocking collectives  294 us (49%)
  waiting for transfers between devices  174 us (29%)
  starting transfers between devices  62.9 us (10%)
  local copies, waits for them, and re-layouts  46.2 us (8%)
  between operations  16.6 us (3%)
  other arithmetic  11.5 us (2%)
    psum x3, blocking collectives, surround(): lat_summed = lax.psum(lat_terms, 'lat')  245 us
    psum x1, waiting for transfers between devices, surround(): lat_summed = lax.psum(lat_terms, 'lat')  142 us
    all_gather x3, blocking collectives, surround(): lon_summed = jnp.sum(lax.all_gather(lon_terms, 'lon'), axis=0)  49.4 us
    ppermute x8, starting transfers between devices, padded_2(): lax.ppermute(head, axis, [((i + 1) % count, i) for i in range(ends)])  31.1 us
    ppermute x8, starting transfers between devices, padded_2(): lax.ppermute(tail, axis, [(i, (i + 1) % count) for i in range(ends)])  20.8 us
    all_gather x1, waiting for transfers between devices, surround(): lon_summed = jnp.sum(lax.all_gather(lon_terms, 'lon'), axis=0)  19.2 us
    gather x16, local copies, waits for them, and re-layouts, rim_terms(): picked = field[jnp.clip(target, 0, rows_dev - 1), cols_at + col_step]  15.7 us
    ppermute x4, waiting for transfers between devices, swapped(): return lax.ppermute(block, axis, route)  12.1 us
  transfers between devices with their start and end apart: 22, of which 6 were waited for; matrix products, arithmetic and copies ran while one was open for 3% of the time, Pallas kernels for 0%

profile of v1, /device:TPU:104, one launch (start us, length us, event | category | flops | bytes accessed | tf_op | source)
XLA Modules:
  0.0 605.0 jit_solution(17411198157895653501)
XLA Ops:
  15.3 3.4 collective-permute-start
  18.8 6.7 %collective-permute-start.1 = (f32[2,32,256]{2,0,1:T(2,128)S(1)}, f32[2,32,256]{2,0,1:T(2,128)S(1)}, u32[]{:S(2)}, u32[]{:S(2)}) collective-permute-start(f32[2,32,256]{2,0,1:T(2,128)S(1)} %get-tuple-element.225), channel_id=1, source_target_pairs={{1,0},{2,1},{3,2},{4,3},{5,4},{6,5},{7,6},{8,7},{9,8},{10,9},{11,1... | collective-permute-start | bytes 196616 | tf_op jit(solution)/shard_map/ppermute | solution.py:23
  34.9 1.9 collective-permute-start.2
  36.9 3.6 collective-permute-start.3
  40.5 19.2 %all-gather.2.cloned.1.call-done = f32[16,2,2,16,256]{4,3,2,1,0:T(8,128)} async-done(((f32[1,2,2,16,256]{4,3,2,1,0:T(8,128)}), f32[16,2,2,16,256]{4,3,2,1,0:T(8,128)}) %all-gather.2.cloned.1.call-update) | async-done | bytes 1048592 | tf_op jit(solution)/shard_map/all_gather | solution.py:79
  61.1 142.1 %all-reduce.12.cloned.1.call-done = f32[2,2,32,256]{3,2,1,0:T(8,128)} async-done(((f32[2,2,32,256]{3,2,1,0:T(8,128)}), f32[2,2,32,256]{3,2,1,0:T(8,128)}) %all-reduce.12.cloned.1.call-update) | async-done | bytes 131088 | tf_op jit(solution)/shard_map/psum | solution.py:78
  204.1 3.4 collective-permute-start.4
  208.8 2.8 collective-permute-done.4
  212.0 1.9 dynamic-slice_select_fusion
  218.2 6.0 collective-permute-start.6
  227.0 1.9 collective-permute-start.5
  232.6 17.2 %all_gather.17 = f32[16,2,1,16,128]{4,3,2,1,0:T(8,128)S(1)} all-gather(f32[1,2,1,16,128]{4,3,2,1,0:T(8,128)S(1)} %multiply_add_fusion.7), channel_id=1, replica_groups=mesh['panel'=2,'lon'=16,'lat'=16] {'lon'}, dimensions={0}, use_global_device_ids=true | all-gather | bytes 278528 | tf_op jit(solution)/shard_map/all_gather | solution.py:79
  249.9 82.9 %psum.29 = f32[2,1,32,128]{3,2,1,0:T(8,128)S(1)} all-reduce(f32[2,1,32,128]{3,2,1,0:T(8,128)S(1)} %multiply_add_fusion.4), channel_id=1, replica_groups=mesh['panel'=2,'lon'=16,'lat'=16] {'lat'}, use_global_device_ids=true, to_apply=%region_3.4 | all-reduce | flops 8192 | bytes 65536 | tf_op jit(solution)/shard_map/psum | solution.py:78
  332.9 1.9 collective-permute-start.7
  334.8 3.6 collective-permute-start.8
  338.5 2.5 collective-permute-start.9
  341.1 3.4 collective-permute-done.9
  354.4 1.9 collective-permute-start.11
  356.3 3.9 collective-permute-start.10
  360.3 16.1 %all_gather.18 = f32[16,2,1,16,128]{4,3,2,1,0:T(8,128)S(1)} all-gather(f32[1,2,1,16,128]{4,3,2,1,0:T(8,128)S(1)} %multiply_add_fusion.6), channel_id=1, replica_groups=mesh['panel'=2,'lon'=16,'lat'=16] {'lon'}, dimensions={0}, use_global_device_ids=true | all-gather | bytes 278528 | tf_op jit(solution)/shard_map/all_gather | solution.py:79
  376.5 80.9 %psum.30 = f32[2,1,32,128]{3,2,1,0:T(8,128)S(1)} all-reduce(f32[2,1,32,128]{3,2,1,0:T(8,128)S(1)} %multiply_add_fusion.3), channel_id=1, replica_groups=mesh['panel'=2,'lon'=16,'lat'=16] {'lat'}, use_global_device_ids=true, to_apply=%region_5.6 | all-reduce | flops 8192 | bytes 65536 | tf_op jit(solution)/shard_map/psum | solution.py:78
  457.5 1.9 collective-permute-start.12
  459.4 3.6 collective-permute-start.13
  463.1 2.5 collective-permute-start.14
  465.7 3.4 collective-permute-done.14
  480.9 3.9 collective-permute-start.15
  484.9 16.1 %all_gather.19 = f32[16,2,1,16,128]{4,3,2,1,0:T(8,128)S(1)} all-gather(f32[1,2,1,16,128]{4,3,2,1,0:T(8,128)S(1)} %multiply_add_fusion.5), channel_id=1, replica_groups=mesh['panel'=2,'lon'=16,'lat'=16] {'lon'}, dimensions={0}, use_global_device_ids=true | all-gather | bytes 278528 | tf_op jit(solution)/shard_map/all_gather | solution.py:79
  501.1 80.9 %psum.31 = f32[2,1,32,128]{3,2,1,0:T(8,128)S(1)} all-reduce(f32[2,1,32,128]{3,2,1,0:T(8,128)S(1)} %multiply_add_fusion.2), channel_id=1, replica_groups=mesh['panel'=2,'lon'=16,'lat'=16] {'lat'}, use_global_device_ids=true, to_apply=%region_7.8 | all-reduce | flops 8192 | bytes 65536 | tf_op jit(solution)/shard_map/psum | solution.py:78
  582.1 1.9 collective-permute-start.17
  584.0 3.6 collective-permute-start.18
  587.7 2.5 collective-permute-start.19
  591.1 2.6 collective-permute-done.19
  (214 shorter events, 57.9 us)
Async XLA Ops:
  8.0 51.8 %all-gather.2.cloned.1.call-start = ((), (), s32[]{:S(2)}) async-start(), calls=%async_computation.1 | async-start | bytes 1114112 | tf_op jit(solution)/shard_map/all_gather | solution.py:79
  8.0 0.7 copy-start.6
  8.1 0.7 copy-start.4
  15.2 187.9 %all-reduce.12.cloned.1.call-start = ((), (), s32[]{:S(2)}) async-start(), calls=%async_computation | async-start | bytes 262144 | tf_op jit(solution)/shard_map/psum | solution.py:78
  15.3 19.6 %collective-permute-start = (f32[2,32,256]{2,0,1:T(2,128)S(1)}, f32[2,32,256]{2,0,1:T(2,128)S(1)}, u32[]{:S(2)}, u32[]{:S(2)}) collective-permute-start(f32[2,32,256]{2,0,1:T(2,128)S(1)} %get-tuple-element.224), channel_id=1, source_target_pairs={{0,1},{1,2},{2,3},{3,4},{4,5},{5,6},{6,7},{7,8},{8,9},{9,10},{10,1... | collective-permute-start | bytes 196616 | tf_op jit(solution)/shard_map/ppermute | solution.py:21
  18.8 16.2 %collective-permute-start.1 = (f32[2,32,256]{2,0,1:T(2,128)S(1)}, f32[2,32,256]{2,0,1:T(2,128)S(1)}, u32[]{:S(2)}, u32[]{:S(2)}) collective-permute-start(f32[2,32,256]{2,0,1:T(2,128)S(1)} %get-tuple-element.225), channel_id=1, source_target_pairs={{1,0},{2,1},{3,2},{4,3},{5,4},{6,5},{7,6},{8,7},{9,8},{10,9},{11,1... | collective-permute-start | bytes 196616 | tf_op jit(solution)/shard_map/ppermute | solution.py:23
  25.4 0.7 copy-start.7
  30.3 1.3 copy-start.5
  32.9 0.7 copy-start.8
  34.9 173.8 %collective-permute-start.2 = (f32[20,2,256]{2,0,1:T(8,128)S(1)}, f32[20,2,256]{2,0,1:T(8,128)S(1)}, u32[]{:S(2)}, u32[]{:S(2)}) collective-permute-start(f32[20,2,256]{2,0,1:T(8,128)S(1)} %get-tuple-element.222), channel_id=1, source_target_pairs={{0,16},{16,32},{32,48},{48,64},{64,80},{80,96},{96,112},{112,128},... | collective-permute-start | bytes 122888 | tf_op jit(solution)/shard_map/ppermute | solution.py:21
  36.9 171.8 %collective-permute-start.3 = (f32[20,2,256]{2,0,1:T(8,128)S(1)}, f32[20,2,256]{2,0,1:T(8,128)S(1)}, u32[]{:S(2)}, u32[]{:S(2)}) collective-permute-start(f32[20,2,256]{2,0,1:T(8,128)S(1)} %get-tuple-element.223), channel_id=1, source_target_pairs={{16,0},{32,16},{48,32},{64,48},{80,64},{96,80},{112,96},{128,112},... | collective-permute-start | bytes 122888 | tf_op jit(solution)/shard_map/ppermute | solution.py:23
  204.1 7.6 %collective-permute-start.4 = (f32[2,2,48,256]{3,2,1,0:T(8,128)S(1)}, f32[2,2,48,256]{3,2,1,0:T(8,128)S(1)}, u32[]{:S(2)}, u32[]{:S(2)}) collective-permute-start(f32[2,2,48,256]{3,2,1,0:T(8,128)S(1)} %pad_maximum_fusion.5), channel_id=1, source_target_pairs={{0,256},{256,0},{1,257},{257,1},{2,258},{258,2},{3,259},{259,3},{4... | collective-permute-start | bytes 589832 | tf_op jit(solution)/shard_map/ppermute | solution.py:37
  216.4 1.0 copy-start
  216.5 1.0 copy-start.1
  218.2 114.7 %collective-permute-start.6 = (f32[1,32,128]{2,0,1:T(1,128)S(1)}, f32[1,32,128]{2,0,1:T(1,128)S(1)}, u32[]{:S(2)}, u32[]{:S(2)}) collective-permute-start(f32[1,32,128]{2,0,1:T(1,128)S(1)} %slice.1083), channel_id=1, source_target_pairs={{1,0},{2,1},{3,2},{4,3},{5,4},{6,5},{7,6},{8,7},{9,8},{10,9},{11,1... | collective-permute-start | bytes 49160 | tf_op jit(solution)/shard_map/ppermute | solution.py:23
  227.0 105.8 %collective-permute-start.5 = (f32[1,32,128]{2,1,0:T(8,128)S(1)}, f32[1,32,128]{2,1,0:T(8,128)S(1)}, u32[]{:S(2)}, u32[]{:S(2)}) collective-permute-start(f32[1,32,128]{2,1,0:T(8,128)S(1)} %slice.1082), channel_id=1, source_target_pairs={{0,1},{1,2},{2,3},{3,4},{4,5},{5,6},{6,7},{7,8},{8,9},{9,10},{10,1... | collective-permute-start | bytes 49160 | tf_op jit(solution)/shard_map/ppermute | solution.py:21
  332.9 8.1 %collective-permute-start.7 = (f32[18,1,128]{2,0,1:T(8,128)S(1)}, f32[18,1,128]{2,0,1:T(8,128)S(1)}, u32[]{:S(2)}, u32[]{:S(2)}) collective-permute-start(f32[18,1,128]{2,0,1:T(8,128)S(1)} %get-tuple-element.230), channel_id=1, source_target_pairs={{0,16},{16,32},{32,48},{48,64},{64,80},{80,96},{96,112},{112,128},... | collective-permute-start | bytes 27656 | tf_op jit(solution)/shard_map/ppermute | solution.py:21
  334.8 6.2 %collective-permute-start.8 = (f32[18,1,128]{2,0,1:T(8,128)S(1)}, f32[18,1,128]{2,0,1:T(8,128)S(1)}, u32[]{:S(2)}, u32[]{:S(2)}) collective-permute-start(f32[18,1,128]{2,0,1:T(8,128)S(1)} %get-tuple-element.231), channel_id=1, source_target_pairs={{16,0},{32,16},{48,32},{64,48},{80,64},{96,80},{112,96},{128,112},... | collective-permute-start | bytes 27656 | tf_op jit(solution)/shard_map/ppermute | solution.py:23
  338.5 6.0 collective-permute-start.9
  346.4 1.0 copy-start.2
  354.4 103.1 %collective-permute-start.11 = (f32[1,32,128]{2,0,1:T(1,128)S(1)}, f32[1,32,128]{2,0,1:T(1,128)S(1)}, u32[]{:S(2)}, u32[]{:S(2)}) collective-permute-start(f32[1,32,128]{2,0,1:T(1,128)S(1)} %slice.1124), channel_id=1, source_target_pairs={{1,0},{2,1},{3,2},{4,3},{5,4},{6,5},{7,6},{8,7},{9,8},{10,9},{11,1... | collective-permute-start | bytes 49160 | tf_op jit(solution)/shard_map/ppermute | solution.py:23
  356.3 101.1 %collective-permute-start.10 = (f32[1,32,128]{2,1,0:T(8,128)S(1)}, f32[1,32,128]{2,1,0:T(8,128)S(1)}, u32[]{:S(2)}, u32[]{:S(2)}) collective-permute-start(f32[1,32,128]{2,1,0:T(8,128)S(1)} %slice.1123), channel_id=1, source_target_pairs={{0,1},{1,2},{2,3},{3,4},{4,5},{5,6},{6,7},{7,8},{8,9},{9,10},{10,1... | collective-permute-start | bytes 49160 | tf_op jit(solution)/shard_map/ppermute | solution.py:21
  457.5 8.1 %collective-permute-start.12 = (f32[18,1,128]{2,0,1:T(8,128)S(1)}, f32[18,1,128]{2,0,1:T(8,128)S(1)}, u32[]{:S(2)}, u32[]{:S(2)}) collective-permute-start(f32[18,1,128]{2,0,1:T(8,128)S(1)} %get-tuple-element.228), channel_id=1, source_target_pairs={{0,16},{16,32},{32,48},{48,64},{64,80},{80,96},{96,112},{112,128},... | collective-permute-start | bytes 27656 | tf_op jit(solution)/shard_map/ppermute | solution.py:21
  459.4 6.2 %collective-permute-start.13 = (f32[18,1,128]{2,0,1:T(8,128)S(1)}, f32[18,1,128]{2,0,1:T(8,128)S(1)}, u32[]{:S(2)}, u32[]{:S(2)}) collective-permute-start(f32[18,1,128]{2,0,1:T(8,128)S(1)} %get-tuple-element.229), channel_id=1, source_target_pairs={{16,0},{32,16},{48,32},{64,48},{80,64},{96,80},{112,96},{128,112},... | collective-permute-start | bytes 27656 | tf_op jit(solution)/shard_map/ppermute | solution.py:23
  463.1 6.0 collective-permute-start.14
  471.0 1.0 copy-start.3
  479.0 103.1 %collective-permute-start.16 = (f32[1,32,128]{2,0,1:T(1,128)S(1)}, f32[1,32,128]{2,0,1:T(1,128)S(1)}, u32[]{:S(2)}, u32[]{:S(2)}) collective-permute-start(f32[1,32,128]{2,0,1:T(1,128)S(1)} %slice.1140), channel_id=1, source_target_pairs={{1,0},{2,1},{3,2},{4,3},{5,4},{6,5},{7,6},{8,7},{9,8},{10,9},{11,1... | collective-permute-start | bytes 49160 | tf_op jit(solution)/shard_map/ppermute | solution.py:23
  480.9 101.1 %collective-permute-start.15 = (f32[1,32,128]{2,1,0:T(8,128)S(1)}, f32[1,32,128]{2,1,0:T(8,128)S(1)}, u32[]{:S(2)}, u32[]{:S(2)}) collective-permute-start(f32[1,32,128]{2,1,0:T(8,128)S(1)} %slice.1139), channel_id=1, source_target_pairs={{0,1},{1,2},{2,3},{3,4},{4,5},{5,6},{6,7},{7,8},{8,9},{9,10},{10,1... | collective-permute-start | bytes 49160 | tf_op jit(solution)/shard_map/ppermute | solution.py:21
  582.1 8.9 %collective-permute-start.17 = (f32[18,1,128]{2,0,1:T(8,128)S(1)}, f32[18,1,128]{2,0,1:T(8,128)S(1)}, u32[]{:S(2)}, u32[]{:S(2)}) collective-permute-start(f32[18,1,128]{2,0,1:T(8,128)S(1)} %get-tuple-element.226), channel_id=1, source_target_pairs={{0,16},{16,32},{32,48},{48,64},{64,80},{80,96},{96,112},{112,128},... | collective-permute-start | bytes 27656 | tf_op jit(solution)/shard_map/ppermute | solution.py:21
  584.0 7.0 %collective-permute-start.18 = (f32[18,1,128]{2,0,1:T(8,128)S(1)}, f32[18,1,128]{2,0,1:T(8,128)S(1)}, u32[]{:S(2)}, u32[]{:S(2)}) collective-permute-start(f32[18,1,128]{2,0,1:T(8,128)S(1)} %get-tuple-element.227), channel_id=1, source_target_pairs={{16,0},{32,16},{48,32},{64,48},{80,64},{96,80},{112,96},{128,112},... | collective-permute-start | bytes 27656 | tf_op jit(solution)/shard_map/ppermute | solution.py:23
  587.7 6.0 collective-permute-start.19
Sparse Core Ops, SparseCore 0:
  15.4 44.3 all-gather.1
Sparse Core Ops, SparseCore 1:
  32.6 170.5 all-reduce.11
